TPU v7x, 512 devices: a whole 4x8x8 slice. The times are simulated.
512 devices in a mesh: segment: 32 (over y_lo, z), dp: 8 (over x, core), seq: 2 (over y_hi).
Axes of the slice: x: 4, y: 8 (y_hi: 2, y_lo: 4; y = y_hi * 4 + y_lo), z: 8, core: 2. Of those that a mesh axis runs over, the one named last changes fastest.
Arguments:
- stored_part_activation: bfloat16 [32, 2, 8, 256, 2048], P('segment', None, 'dp', 'seq'), may hold values from -64 to 64
- pending_sensitivity: bfloat16 [32, 8, 256, 2048], P('segment', 'dp', 'seq'), may hold values from -0.119628906 to 0.119628906
- uppermost_result_derivative: bfloat16 [1, 8, 256, 2048], P(None, 'dp', 'seq'), may hold values from -0.119628906 to 0.119628906
- scaling_factors: float32 [32, 4, 2048], P('segment'), may hold values from -0.5 to 5
- attended_tile_table: int32 [32, 2, 8, 2, 2], P('segment', None, 'dp'), may hold values from 0 to 1, as said below
- active_tile_number: int32 [32, 2, 8, 2], P('segment', None, 'dp'), may hold values from 1 to 2
Outputs:
- factor_derivatives: float32 [32, 4, 2048], P('segment')
Inputs may be any that keep to these rules, and one draw needn't show every extreme that they name: `attended_tile_table`: each list names every key block of its sample once; the allowed ones come first.
All inputs are finite; a program needn't handle non-finite values.
Results may differ from a plain program's by a relative error of at most 0.009.
Values may be sent and summed in bfloat16 or wider, within the bound.
A program may use at most 64 MiB of HBM per device.

v0:
```python
import jax
import jax.numpy as jnp
from jax import lax
from jax.sharding import PartitionSpec as P

HEAD_DIM = 128
BLK = 128
epsilon = 1e-06


def partner(block, axis, apart):
    count = lax.axis_size(axis)
    route = []
    for low in range(count):
        high = low | 1 << apart
        if high != low and high < count:
            route += [(low, high), (high, low)]
    return lax.ppermute(block, axis, route)


def from_behind(block, axis, distance):
    devices = range(lax.axis_size(axis))
    route = [(i - distance, i) for i in devices if i - distance in devices]
    return lax.ppermute(block, axis, route)


def normed_of(inputs):
    widened = inputs.astype(jnp.float32).reshape(
        inputs.shape[:-1] + (inputs.shape[-1] // HEAD_DIM, HEAD_DIM)
    )
    inv_rms = lax.rsqrt(jnp.mean(widened * widened, axis=-1, keepdims=True) + epsilon)
    return (widened * inv_rms, inv_rms)


def norm_back(grad_norm, norm_val, inv_rms):
    return inv_rms * (grad_norm - norm_val * jnp.mean(grad_norm * norm_val, axis=-1, keepdims=True))


def allowed_blocks(block_list, live_count):
    block_total = block_list.shape[0]
    live_slots = jnp.arange(block_total)[None, :] < live_count[:, None]
    matches = (block_list[:, :, None] == jnp.arange(block_total)[None, None, :]) & live_slots[
        :, :, None
    ]
    return jnp.any(matches, axis=1)


def token_mask(permitted, query_half, seq_index, dev_blocks):
    local_blocks = jnp.arange(dev_blocks, dtype=jnp.int32)
    query_rows = query_half * dev_blocks + local_blocks
    key_order = jnp.concatenate(
        [seq_index * dev_blocks + local_blocks, (1 - seq_index) * dev_blocks + local_blocks]
    )
    picked = permitted[query_rows[:, None], key_order[None, :]]
    return jnp.repeat(jnp.repeat(picked, BLK, axis=0), BLK, axis=1)


def attend(query_norm, key_norm, gain_heads, allowed, incoming, scaling):
    queries = (query_norm * gain_heads[0]).astype(jnp.bfloat16)
    key_mat = (key_norm * gain_heads[1]).astype(jnp.bfloat16)
    val_mat = (key_norm * gain_heads[2]).astype(jnp.bfloat16)
    scores = (
        jnp.einsum("thd,shd->hts", queries, key_mat, preferred_element_type=jnp.float32) * scaling
    )
    scores = jnp.where(allowed[None], scores, -jnp.inf)
    exped = jnp.exp(scores - jnp.max(scores, axis=-1, keepdims=True))
    probs = exped / jnp.sum(exped, axis=-1, keepdims=True)
    probs_low = probs.astype(jnp.bfloat16)
    output = jnp.einsum("hts,shd->thd", probs_low, val_mat, preferred_element_type=jnp.float32)
    grad_out = (gain_heads[3] * incoming).astype(jnp.bfloat16)
    grad_probs = jnp.einsum("thd,shd->hts", grad_out, val_mat, preferred_element_type=jnp.float32)
    grad_scores = (
        probs * (grad_probs - jnp.sum(probs * grad_probs, axis=-1, keepdims=True))
    ).astype(jnp.bfloat16)
    return (queries, key_mat, probs_low, output, grad_out, grad_scores)


def shards(
    stored_part_activation,
    pending_sensitivity,
    uppermost_result_derivative,
    scaling_factors,
    attended_tile_table,
    active_tile_number,
):
    segments = lax.axis_size("segment")
    segment_index = lax.axis_index("segment")
    seq_index = lax.axis_index("seq")
    window = stored_part_activation.shape[1]
    row_count = stored_part_activation.shape[3]
    channels = stored_part_activation.shape[4]
    head_count = channels // HEAD_DIM
    dev_blocks = row_count // BLK
    scaling = HEAD_DIM ** (-0.5)
    own_window = stored_part_activation[0, :, 0]
    gain_heads = scaling_factors[0].reshape(4, head_count, HEAD_DIM)
    incoming_sensitivity = pending_sensitivity[0, 0].astype(jnp.float32)
    totals = jnp.zeros((4, head_count, HEAD_DIM), jnp.float32)
    for step_index in range(window):
        own_rows = own_window[step_index]
        other_rows = partner(own_rows, "seq", 0)
        permitted = allowed_blocks(
            attended_tile_table[0, step_index, 0], active_tile_number[0, step_index, 0]
        )
        own_norm, own_inv = normed_of(own_rows)
        other_norm, other_inv = normed_of(other_rows)
        key_norm = jnp.concatenate([own_norm, other_norm], axis=0)
        incoming = incoming_sensitivity.reshape(row_count, head_count, HEAD_DIM)
        own_allowed = token_mask(permitted, seq_index, seq_index, dev_blocks)
        queries, key_mat, probs_low, output, grad_out, grad_scores = attend(
            own_norm, key_norm, gain_heads, own_allowed, incoming, scaling
        )
        grad_query = (
            jnp.einsum("hts,shd->thd", grad_scores, key_mat, preferred_element_type=jnp.float32)
            * scaling
        )
        grad_key = (
            jnp.einsum("hts,thd->shd", grad_scores, queries, preferred_element_type=jnp.float32)
            * scaling
        )
        grad_value = jnp.einsum(
            "hts,thd->shd", probs_low, grad_out, preferred_element_type=jnp.float32
        )
        key_part = grad_key * gain_heads[1] + grad_value * gain_heads[2]
        self_part = key_part[:row_count]
        key_terms = jnp.sum(grad_key * key_norm, axis=0)
        value_terms = jnp.sum(grad_value * key_norm, axis=0)
        if step_index < window - 1:
            lent = norm_back(key_part[row_count:], other_norm, other_inv).astype(jnp.bfloat16)
            returned = partner(lent, "seq", 0).astype(jnp.float32)
        grad_terms = jnp.stack(
            [
                jnp.sum(grad_query * own_norm, axis=0),
                key_terms,
                value_terms,
                jnp.sum(output * incoming, axis=0),
            ]
        )
        totals = totals + grad_terms
        if step_index < window - 1:
            grad_input = (
                incoming
                + norm_back(grad_query * gain_heads[0] + self_part, own_norm, own_inv)
                + returned
            )
            received = from_behind(grad_input.reshape(row_count, channels), "segment", -1)
            incoming_sensitivity = jnp.where(
                segment_index == segments - 1,
                uppermost_result_derivative[step_index, 0].astype(jnp.float32),
                received,
            )
    summed = lax.psum(totals.reshape(4, channels), ("dp", "seq"))
    return summed[None]


def solution(mesh):
    placed = (
        P("segment", None, "dp", "seq", None),
        P("segment", "dp", "seq", None),
        P(None, "dp", "seq", None),
        P("segment", None, None),
        P("segment", None, "dp", None, None),
        P("segment", None, "dp", None),
    )
    return jax.shard_map(
        shards, mesh=mesh, in_specs=placed, out_specs=P("segment", None, None), check_vma=False
    )
```

profile of v0, /device:TPU:24, one launch (start us, length us, event | category | flops | bytes accessed | tf_op | source)
XLA Modules:
  0.0 220.2 jit_solution(2187491883206557950)
XLA Ops:
  0.0 2.7 %slice_convert_fusion = (f32[1,1,1,128,2048]{4,3,2,1,0:T(8,128)}, bf16[128,2048]{1,0:T(8,128)(2,1)}, bf16[128,2048]{1,0:T(8,128)(2,1)}, f32[1,1,1,128,2048]{4,3,2,1,0:T(8,128)S(1)}) fusion(bf16[1,2,1,128,2048]{4,3,2,1,0:T(8,128)(2,1)} %param.6), kind=kLoop, calls=%fused_computation.75 | loop fusion | flops 524288 | bytes 4194304 | tf_op jit(solution)/shard_map/convert_element_type | solution.py:28
  2.7 5.0 %collective-permute-start = (bf16[128,2048]{1,0:T(8,128)(2,1)}, bf16[128,2048]{1,0:T(8,128)(2,1)}, u32[]{:S(2)}, u32[]{:S(2)}) collective-permute-start(bf16[128,2048]{1,0:T(8,128)(2,1)} %get-tuple-element.12), channel_id=1, source_target_pairs={{0,1},{1,0},{2,3},{3,2},{4,5},{5,4},{6,7},{7,6},{8,9},{9,8},{10,11... | collective-permute-start | bytes 1572872 | tf_op jit(solution)/shard_map/ppermute | solution.py:18
  7.8 4.7 %collective-permute-start.1 = (bf16[128,2048]{1,0:T(8,128)(2,1)}, bf16[128,2048]{1,0:T(8,128)(2,1)}, u32[]{:S(2)}, u32[]{:S(2)}) collective-permute-start(bf16[128,2048]{1,0:T(8,128)(2,1)} %get-tuple-element.13), channel_id=1, source_target_pairs={{0,1},{1,0},{2,3},{3,2},{4,5},{5,4},{6,7},{7,6},{8,9},{9,8},{10,11... | collective-permute-start | bytes 1572872 | tf_op jit(solution)/shard_map/ppermute | solution.py:18
  12.6 0.2 or_reduce_fusion
  12.9 0.1 and_reduce_fusion.1
  13.0 0.6 gather_fusion
  13.7 0.3 copy.49
  14.1 0.1 broadcast_multiply_fusion.3
  14.2 0.6 copy-done.11
  14.8 1.5 copy.58
  16.4 0.1 multiply_reduce_fusion.5
  16.5 0.1 and_reduce_fusion
  16.6 2.3 %copy.53 = f32[1,1,128,2048]{2,3,1,0:T(8,128)} copy(bf16[1,1,128,2048]{3,2,1,0:T(8,128)(2,1)} %param.7) | data formatting | bytes 1572864 | tf_op jit(solution)/shard_map/convert_element_type | solution.py:97
  18.9 0.6 gather_fusion.1
  19.5 1.1 broadcast_multiply_fusion.1
  20.6 12.6 %collective-permute-done = bf16[128,2048]{1,0:T(8,128)(2,1)} collective-permute-done((bf16[128,2048]{1,0:T(8,128)(2,1)}, bf16[128,2048]{1,0:T(8,128)(2,1)}, u32[]{:S(2)}, u32[]{:S(2)}) %collective-permute-start) | collective-permute-done | bytes 524320 | tf_op jit(solution)/shard_map/ppermute | solution.py:18
  33.2 1.2 copy.50
  34.5 1.1 broadcast_multiply_fusion.2
  35.6 3.9 %fusion.49 = (f32[16,128]{1,0:T(8,128)S(1)}, f32[16,128,256]{2,1,0:T(8,128)}) fusion(pred[256]{0:T(512)(128)(4,1)S(1)} %broadcast_bitcast_fusion.1, f32[16,128]{1,0:T(8,128)S(1)} %bitcast.124, f32[128,16,128]{0,2,1:T(8,128)} %broadcast_multiply_fusion.2, f32[128,16,128]{0,2,1:T(8,128)S(1)} %broadcast_multiply_fusion.3, f32[16,128]{1,0:T(8,128)S(1)} %bitcast.119), kind=kOutput, calls=%fused_computation.119 | convolution fusion | flops 138412288 | bytes 4219136 | tf_op jit(solution)/shard_map/sub | solution.py:66
  39.5 2.8 %fusion.26 = f32[16,128,256]{2,1,0:T(8,128)S(1)} fusion(f32[128,16,128]{0,2,1:T(8,128)} %bitcast.110, f32[16,128]{1,0:T(8,128)S(1)} %bitcast.141, f32[16,128,256]{2,1,0:T(8,128)} %get-tuple-element.24, f32[16,128]{1,0:T(8,128)S(1)} %get-tuple-element.23), kind=kOutput, calls=%fused_computation.70 | convolution fusion | flops 135790592 | bytes 5259264 | tf_op jit(solution)/shard_map/hts,thd->shd/dot_general | solution.py:121
  42.4 0.3 copy-done.5
  42.7 2.2 multiply_reduce_fusion.1
  44.9 0.7 multiply_convert_fusion.3
  45.6 1.9 fusion.5
  47.6 1.9 multiply_reduce_fusion.3
  49.5 1.0 multiply_convert_fusion.7
  50.5 6.3 %collective-permute-start.2 = (bf16[128,16,128]{0,2,1:T(8,128)(2,1)}, bf16[128,16,128]{0,2,1:T(8,128)(2,1)}, u32[]{:S(2)}, u32[]{:S(2)}) collective-permute-start(bf16[128,16,128]{0,2,1:T(8,128)(2,1)} %multiply_convert_fusion.7), channel_id=1, source_target_pairs={{0,1},{1,0},{2,3},{3,2},{4,5},{5,4},{6,7},{7,6},{8,9},{9,8},{10,11... | collective-permute-start | bytes 1572872 | tf_op jit(solution)/shard_map/ppermute | solution.py:18
  56.9 1.2 copy.59
  58.2 22.9 %collective-permute-done.2 = bf16[128,16,128]{0,2,1:T(8,128)(2,1)} collective-permute-done((bf16[128,16,128]{0,2,1:T(8,128)(2,1)}, bf16[128,16,128]{0,2,1:T(8,128)(2,1)}, u32[]{:S(2)}, u32[]{:S(2)}) %collective-permute-start.2) | collective-permute-done | bytes 524320 | tf_op jit(solution)/shard_map/ppermute | solution.py:18
  81.1 3.6 %convert_add_fusion = f32[128,16,128]{0,2,1:T(8,128)} fusion(bf16[128,16,128]{0,2,1:T(8,128)(2,1)} %collective-permute-done.2, f32[128,16,128]{0,2,1:T(8,128)} %bitcast.111, f32[128,16]{0,1:T(8,128)S(1)} %broadcast_multiply_fusion.7, f32[128,16]{0,1:T(8,128)S(1)} %add_rsqrt_fusion.3, f32[256,16,128]{0,2,1:T(8,128)} %copy-done.2, ...), kind=kLoop, calls=%fused_computation.45 | loop fusion | flops 2359296 | bytes 5791744 | tf_op jit(solution)/shard_map/add | solution.py:142
  84.7 2.6 %copy.62 = f32[128,2048]{1,0:T(8,128)} copy(f32[128,2048]{0,1:T(8,128)} %bitcast.114) | data formatting | bytes 2097152 | tf_op jit(solution)/shard_map/reshape | solution.py:146
  87.3 11.7 %collective-permute-start.3 = (f32[128,2048]{1,0:T(8,128)}, f32[128,2048]{1,0:T(8,128)}, u32[]{:S(2)}, u32[]{:S(2)}) collective-permute-start(f32[128,2048]{1,0:T(8,128)} %copy.62), channel_id=1, source_target_pairs={{16,0},{32,16},{48,32},{64,48},{80,64},{96,80},{112,96},{128,112},... | collective-permute-start | bytes 3145736 | tf_op jit(solution)/shard_map/ppermute | solution.py:24
  99.0 1.1 broadcast_multiply_fusion
  100.1 4.8 %fusion.50 = (f32[16,128]{1,0:T(8,128)S(1)}, f32[16,128,256]{2,1,0:T(8,128)}) fusion(pred[256]{0:T(512)(128)(4,1)S(1)} %broadcast_bitcast_fusion, f32[16,128]{1,0:T(8,128)S(1)} %bitcast.126, f32[128,16,128]{0,2,1:T(8,128)} %broadcast_multiply_fusion, f32[128,16,128]{0,2,1:T(8,128)} %broadcast_multiply_fusion.1, f32[16,128]{1,0:T(8,128)S(1)} %bitcast.121), kind=kOutput, calls=%fused_computation.120 | convolution fusion | flops 138412288 | bytes 4219136 | tf_op jit(solution)/shard_map/sub | solution.py:66
  104.9 2.6 %fusion.12 = f32[16,128]{1,0:T(8,128)S(1)} fusion(f32[128,16,128]{0,2,1:T(8,128)S(1)} %bitcast.113, f32[16,128]{1,0:T(8,128)S(1)} %bitcast.133, f32[128,16,128]{0,2,1:T(8,128)S(1)} %copy-done.1, f32[128,16,128]{0,2,1:T(8,128)S(1)} %broadcast_multiply_fusion.3, f32[16,128,256]{2,1,0:T(8,128)} %get-tuple-element.24, f32[16,128]{1,0:T(8,128)S(1)} %get-tuple-element.23), kind=kOutput, calls=%fused_computation.37 | convolution fusion | flops 137361408 | bytes 5267456 | tf_op jit(solution)/shard_map/hts,shd->thd/dot_general | solution.py:69
  107.5 14.2 %collective-permute-done.3 = f32[128,2048]{1,0:T(8,128)} collective-permute-done((f32[128,2048]{1,0:T(8,128)}, f32[128,2048]{1,0:T(8,128)}, u32[]{:S(2)}, u32[]{:S(2)}) %collective-permute-start.3) | collective-permute-done | bytes 1048608 | tf_op jit(solution)/shard_map/ppermute | solution.py:24
  121.7 1.3 convert_select_fusion
  123.1 1.3 copy.63
  124.4 3.4 %multiply_reduce_fusion = (f32[16,128]{1,0:T(8,128)S(1)}, f32[16,128,256]{2,1,0:T(8,128)S(1)}) fusion(f32[16,128,256]{2,1,0:T(8,128)S(1)} %copy-done.6, f32[16,128]{1,0:T(8,128)S(1)} %get-tuple-element.28, f32[16,128]{1,0:T(8,128)S(1)} %bitcast.134, f32[128,16,128]{0,2,1:T(8,128)} %broadcast_multiply_fusion, f32[128,16,128]{0,2,1:T(8,128)} %broadcast_multiply_fusion.1, ...), kind=kOutput, calls=%fused_computation.17 | convolution fusion | flops 137885696 | bytes 7372800 | tf_op jit(solution)/shard_map/thd,shd->hts/dot_general | solution.py:71
  127.8 0.8 multiply_convert_fusion
  128.6 0.4 copy-done.7
  129.0 0.3 copy-done.8
  129.4 0.7 fusion.13
  130.0 0.7 fusion.3
  130.7 0.5 copy-done.9
  131.3 1.1 fusion.2
  132.4 1.2 fusion.14
  133.7 86.5 %psum.7 = f32[1,4,2048]{2,1,0:T(4,128)} all-reduce(f32[1,4,2048]{2,1,0:T(4,128)S(1)} %fusion.32), channel_id=1, replica_groups=mesh['segment'=32,'dp'=8,'seq'=2] {'dp','seq'}, use_global_device_ids=true, to_apply=%region_22.23 | all-reduce | flops 8192 | bytes 65536 | tf_op jit(solution)/shard_map/psum | solution.py:152
  (44 shorter events, 0.8 us)
Async XLA Ops:
  0.0 12.8 %copy-start.13 = (s32[1,2,1,2]{3,2,1,0:T(1,128)S(1)}, s32[1,2,1,2]{3,2,1,0:T(1,128)}, u32[]{:S(2)}) copy-start(s32[1,2,1,2]{3,2,1,0:T(1,128)} %param.11) | copy-start | bytes 52
  0.0 12.8 %copy-start.12 = (s32[1,2,1,2,2]{4,3,2,1,0:T(2,128)S(1)}, s32[1,2,1,2,2]{4,3,2,1,0:T(2,128)}, u32[]{:S(2)}) copy-start(s32[1,2,1,2,2]{4,3,2,1,0:T(2,128)} %param.10) | copy-start | bytes 100
  2.7 30.5 %collective-permute-start = (bf16[128,2048]{1,0:T(8,128)(2,1)}, bf16[128,2048]{1,0:T(8,128)(2,1)}, u32[]{:S(2)}, u32[]{:S(2)}) collective-permute-start(bf16[128,2048]{1,0:T(8,128)(2,1)} %get-tuple-element.12), channel_id=1, source_target_pairs={{0,1},{1,0},{2,3},{3,2},{4,5},{5,4},{6,7},{7,6},{8,9},{9,8},{10,11... | collective-permute-start | bytes 1572872 | tf_op jit(solution)/shard_map/ppermute | solution.py:18
  7.8 49.1 %collective-permute-start.1 = (bf16[128,2048]{1,0:T(8,128)(2,1)}, bf16[128,2048]{1,0:T(8,128)(2,1)}, u32[]{:S(2)}, u32[]{:S(2)}) collective-permute-start(bf16[128,2048]{1,0:T(8,128)(2,1)} %get-tuple-element.13), channel_id=1, source_target_pairs={{0,1},{1,0},{2,3},{3,2},{4,5},{5,4},{6,7},{7,6},{8,9},{9,8},{10,11... | collective-permute-start | bytes 1572872 | tf_op jit(solution)/shard_map/ppermute | solution.py:18
  14.0 0.8 copy-start.11
  39.5 2.9 %copy-start = (f32[128,16,128]{0,2,1:T(8,128)S(1)}, f32[128,16,128]{0,2,1:T(8,128)}, u32[]{:S(2)}) copy-start(f32[128,16,128]{0,2,1:T(8,128)} %broadcast_multiply_fusion.2) | copy-start | bytes 3145732
  39.5 2.9 %copy-start.3 = (f32[1,1,128,2048]{2,3,1,0:T(8,128)S(1)}, f32[1,1,128,2048]{2,3,1,0:T(8,128)}, u32[]{:S(2)}) copy-start(f32[1,1,128,2048]{2,3,1,0:T(8,128)} %copy.53) | copy-start | bytes 3145732
  39.5 3.2 %copy-start.5 = (f32[16,128,256]{2,1,0:T(8,128)S(1)}, f32[16,128,256]{2,1,0:T(8,128)}, u32[]{:S(2)}) copy-start(f32[16,128,256]{2,1,0:T(8,128)} %get-tuple-element.24) | copy-start | bytes 6291460
  47.6 1.9 copy-start.2
  50.5 30.6 %collective-permute-start.2 = (bf16[128,16,128]{0,2,1:T(8,128)(2,1)}, bf16[128,16,128]{0,2,1:T(8,128)(2,1)}, u32[]{:S(2)}, u32[]{:S(2)}) collective-permute-start(bf16[128,16,128]{0,2,1:T(8,128)(2,1)} %multiply_convert_fusion.7), channel_id=1, source_target_pairs={{0,1},{1,0},{2,3},{3,2},{4,5},{5,4},{6,7},{7,6},{8,9},{9,8},{10,11... | collective-permute-start | bytes 1572872 | tf_op jit(solution)/shard_map/ppermute | solution.py:18
  87.3 34.4 %collective-permute-start.3 = (f32[128,2048]{1,0:T(8,128)}, f32[128,2048]{1,0:T(8,128)}, u32[]{:S(2)}, u32[]{:S(2)}) collective-permute-start(f32[128,2048]{1,0:T(8,128)} %copy.62), channel_id=1, source_target_pairs={{16,0},{32,16},{48,32},{64,48},{80,64},{96,80},{112,96},{128,112},... | collective-permute-start | bytes 3145736 | tf_op jit(solution)/shard_map/ppermute | solution.py:24
  100.1 4.8 %copy-start.1 = (f32[128,16,128]{0,2,1:T(8,128)S(1)}, f32[128,16,128]{0,2,1:T(8,128)}, u32[]{:S(2)}) copy-start(f32[128,16,128]{0,2,1:T(8,128)} %broadcast_multiply_fusion.2) | copy-start | bytes 3145732
  100.1 4.8 %copy-start.4 = (f32[1,1,128,2048]{2,3,1,0:T(8,128)S(1)}, f32[1,1,128,2048]{2,3,1,0:T(8,128)}, u32[]{:S(2)}) copy-start(f32[1,1,128,2048]{2,3,1,0:T(8,128)} %copy.53) | copy-start | bytes 3145732
  104.9 16.8 %copy-start.10 = (bf16[1,1,128,2048]{3,2,1,0:T(8,128)(2,1)S(1)}, bf16[1,1,128,2048]{3,2,1,0:T(8,128)(2,1)}, u32[]{:S(2)}) copy-start(bf16[1,1,128,2048]{3,2,1,0:T(8,128)(2,1)} %param.8) | copy-start | bytes 1572868
  107.5 16.9 %copy-start.6 = (f32[16,128,256]{2,1,0:T(8,128)S(1)}, f32[16,128,256]{2,1,0:T(8,128)}, u32[]{:S(2)}) copy-start(f32[16,128,256]{2,1,0:T(8,128)} %get-tuple-element.29) | copy-start | bytes 6291460
  127.8 1.2 copy-start.7
  127.8 1.5 copy-start.8
  130.0 1.2 copy-start.9
where the time goes:
time: 221 us; the launch traced here: 220 us
  blocking collectives  86.5 us (39%)
  waiting for transfers between devices  49.7 us (22%)
  starting transfers between devices  27.7 us (13%)
  matrix products  27.2 us (12%)
  other arithmetic  14.5 us (7%)
  local copies, waits for them, and re-layouts  14.3 us (6%)
    psum x1, blocking collectives, shards(): summed = lax.psum(totals.reshape(4, channels), ('dp', 'seq'))  86.5 us
    ppermute x3, waiting for transfers between devices, partner(): return lax.ppermute(block, axis, route)  35.5 us
    ppermute x3, starting transfers between devices, partner(): return lax.ppermute(block, axis, route)  16 us
    ppermute x1, waiting for transfers between devices, from_behind(): return lax.ppermute(block, axis, route)  14.2 us
    ppermute x1, starting transfers between devices, from_behind(): return lax.ppermute(block, axis, route)  11.7 us
    sub x2, matrix products, attend(): exped = jnp.exp(scores - jnp.max(scores, axis=-1, keepdims=True))  8.66 us
    dot_general x2, matrix products, attend(): jnp.einsum('thd,shd->hts', grad_out, val_mat, preferred_element_type=jnp....  5.55 us
  transfers between devices with their start and end apart: 4, of which 3 were waited for; matrix products, arithmetic and copies ran while one was open for 16% of the time, Pallas kernels for 0%

commit v1 on v0

--- a/solution.py
+++ b/solution.py
@@ -149,7 +149,7 @@
                 uppermost_result_derivative[step_index, 0].astype(jnp.float32),
                 received,
             )
-    summed = lax.psum(totals.reshape(4, channels), ("dp", "seq"))
+    summed = lax.psum(lax.psum(totals.reshape(4, channels), "dp"), "seq")
     return summed[None]
 
 

time: 221 us -> 174 us (0.79)
  the two profiles are of different devices: /device:TPU:24 before, /device:TPU:56 now
where the time goes in v1:
time: 174 us; the launch traced here: 173 us
  waiting for transfers between devices  51 us (29%)
  blocking collectives  40.7 us (23%)
  matrix products  27.2 us (16%)
  starting transfers between devices  24.9 us (14%)
  other arithmetic  14.5 us (8%)
  local copies, waits for them, and re-layouts  14.3 us (8%)
    psum x2, blocking collectives, shards(): summed = lax.psum(lax.psum(totals.reshape(4, channels), 'dp'), 'seq')  40.7 us
    ppermute x3, waiting for transfers between devices, partner(): return lax.ppermute(block, axis, route)  37.9 us
    ppermute x3, starting transfers between devices, partner(): return lax.ppermute(block, axis, route)  13.2 us
    ppermute x1, waiting for transfers between devices, from_behind(): return lax.ppermute(block, axis, route)  13.1 us
    ppermute x1, starting transfers between devices, from_behind(): return lax.ppermute(block, axis, route)  11.7 us
    sub x2, matrix products, attend(): exped = jnp.exp(scores - jnp.max(scores, axis=-1, keepdims=True))  8.66 us
    dot_general x2, matrix products, attend(): jnp.einsum('thd,shd->hts', grad_out, val_mat, preferred_element_type=jnp....  5.55 us
    dot_general x2, matrix products, shards(): jnp.einsum('hts,thd->shd', probs_low, grad_out, preferred_element_type=jn...  4 us
  transfers between devices with their start and end apart: 4, of which 3 were waited for; matrix products, arithmetic and copies ran while one was open for 20% of the time, Pallas kernels for 0%

profile of v1, /device:TPU:56, one launch (start us, length us, event | category | flops | bytes accessed | tf_op | source)
XLA Modules:
  0.0 172.8 jit_solution(13839083386566418701)
XLA Ops:
  0.0 2.7 %slice_convert_fusion = (f32[1,1,1,128,2048]{4,3,2,1,0:T(8,128)}, bf16[128,2048]{1,0:T(8,128)(2,1)}, bf16[128,2048]{1,0:T(8,128)(2,1)}, f32[1,1,1,128,2048]{4,3,2,1,0:T(8,128)S(1)}) fusion(bf16[1,2,1,128,2048]{4,3,2,1,0:T(8,128)(2,1)} %param.6), kind=kLoop, calls=%fused_computation.75 | loop fusion | flops 524288 | bytes 4194304 | tf_op jit(solution)/shard_map/convert_element_type | solution.py:28
  2.7 4.7 %collective-permute-start = (bf16[128,2048]{1,0:T(8,128)(2,1)}, bf16[128,2048]{1,0:T(8,128)(2,1)}, u32[]{:S(2)}, u32[]{:S(2)}) collective-permute-start(bf16[128,2048]{1,0:T(8,128)(2,1)} %get-tuple-element.12), channel_id=1, source_target_pairs={{0,1},{1,0},{2,3},{3,2},{4,5},{5,4},{6,7},{7,6},{8,9},{9,8},{10,11... | collective-permute-start | bytes 1572872 | tf_op jit(solution)/shard_map/ppermute | solution.py:18
  7.4 5.0 %collective-permute-start.1 = (bf16[128,2048]{1,0:T(8,128)(2,1)}, bf16[128,2048]{1,0:T(8,128)(2,1)}, u32[]{:S(2)}, u32[]{:S(2)}) collective-permute-start(bf16[128,2048]{1,0:T(8,128)(2,1)} %get-tuple-element.13), channel_id=1, source_target_pairs={{0,1},{1,0},{2,3},{3,2},{4,5},{5,4},{6,7},{7,6},{8,9},{9,8},{10,11... | collective-permute-start | bytes 1572872 | tf_op jit(solution)/shard_map/ppermute | solution.py:18
  12.6 0.2 or_reduce_fusion
  12.9 0.1 and_reduce_fusion.1
  13.0 0.6 gather_fusion
  13.7 0.3 copy.49
  14.1 0.1 broadcast_multiply_fusion.3
  14.2 0.6 copy-done.11
  14.8 1.5 copy.58
  16.5 0.1 and_reduce_fusion
  16.6 2.3 %copy.53 = f32[1,1,128,2048]{2,3,1,0:T(8,128)} copy(bf16[1,1,128,2048]{3,2,1,0:T(8,128)(2,1)} %param.7) | data formatting | bytes 1572864 | tf_op jit(solution)/shard_map/convert_element_type | solution.py:97
  18.9 0.6 gather_fusion.1
  19.5 1.1 broadcast_multiply_fusion.1
  20.6 13.8 %collective-permute-done = bf16[128,2048]{1,0:T(8,128)(2,1)} collective-permute-done((bf16[128,2048]{1,0:T(8,128)(2,1)}, bf16[128,2048]{1,0:T(8,128)(2,1)}, u32[]{:S(2)}, u32[]{:S(2)}) %collective-permute-start) | collective-permute-done | bytes 524320 | tf_op jit(solution)/shard_map/ppermute | solution.py:18
  34.4 1.2 copy.50
  35.8 1.1 broadcast_multiply_fusion.2
  36.9 3.9 %fusion.48 = (f32[16,128]{1,0:T(8,128)S(1)}, f32[16,128,256]{2,1,0:T(8,128)}) fusion(pred[256]{0:T(512)(128)(4,1)S(1)} %broadcast_bitcast_fusion.1, f32[16,128]{1,0:T(8,128)S(1)} %bitcast.124, f32[128,16,128]{0,2,1:T(8,128)} %broadcast_multiply_fusion.2, f32[128,16,128]{0,2,1:T(8,128)S(1)} %broadcast_multiply_fusion.3, f32[16,128]{1,0:T(8,128)S(1)} %bitcast.119), kind=kOutput, calls=%fused_computation.118 | convolution fusion | flops 138412288 | bytes 4219136 | tf_op jit(solution)/shard_map/sub | solution.py:66
  40.8 2.8 %fusion.26 = f32[16,128,256]{2,1,0:T(8,128)S(1)} fusion(f32[128,16,128]{0,2,1:T(8,128)} %bitcast.109, f32[16,128]{1,0:T(8,128)S(1)} %bitcast.141, f32[16,128,256]{2,1,0:T(8,128)} %get-tuple-element.24, f32[16,128]{1,0:T(8,128)S(1)} %get-tuple-element.23), kind=kOutput, calls=%fused_computation.70 | convolution fusion | flops 135790592 | bytes 5259264 | tf_op jit(solution)/shard_map/hts,thd->shd/dot_general | solution.py:121
  43.6 0.3 copy-done.5
  43.9 2.2 %multiply_reduce_fusion.1 = (f32[16,128]{1,0:T(8,128)S(1)}, f32[16,128,256]{2,1,0:T(8,128)S(1)}) fusion(f32[16,128,256]{2,1,0:T(8,128)S(1)} %copy-done.5, f32[16,128]{1,0:T(8,128)S(1)} %get-tuple-element.23, f32[16,128]{1,0:T(8,128)S(1)} %bitcast.131, f32[128,16,128]{0,2,1:T(8,128)S(1)} %copy-done, f32[128,16,128]{0,2,1:T(8,128)S(1)} %broadcast_multiply_fusion.3, ...), kind=kOutput, calls=%fused_computation.23 | convolution fusion | flops 137885696 | bytes 7372800 | tf_op jit(solution)/shard_map/thd,shd->hts/dot_general | solution.py:71
  46.1 0.7 multiply_convert_fusion.3
  46.9 1.9 %fusion.5 = (f32[16,128]{1,0:T(8,128)S(1)}, f32[16,128]{1,0:T(8,128)S(1)}, f32[256,16,128]{0,2,1:T(8,128)S(1)}) fusion(f32[128,16,128]{0,2,1:T(8,128)S(1)} %copy-done, f32[128,16,128]{0,2,1:T(8,128)S(1)} %broadcast_multiply_fusion.3, f32[16,128,256]{2,1,0:T(8,128)S(1)} %fusion.26, f32[16,128]{1,0:T(8,128)S(1)} %bitcast.132, ...), kind=kOutput, calls=%fused_computation.15 | convolution fusion | flops 139456512 | bytes 7380992 | tf_op jit(solution)/shard_map/hts,thd->shd/dot_general | solution.py:118
  48.8 1.9 %multiply_reduce_fusion.3 = (f32[128,16]{0,1:T(8,128)S(1)}, f32[128,16]{0,1:T(8,128)S(1)}, f32[16,128]{1,0:T(8,128)S(1)}, f32[16,128,128]{2,1,0:T(8,128)}) fusion(f32[128,16,128]{0,2,1:T(8,128)S(1)} %broadcast_multiply_fusion.3, f32[256,16,128]{0,2,1:T(8,128)S(1)} %get-tuple-element.10, f32[16,128]{1,0:T(8,128)S(1)} %broadcast_multiply_fusion.5, ...), kind=kOutput, calls=%fused_computation.48 | convolution fusion | flops 138143744 | bytes 8429568 | tf_op jit(solution)/shard_map/hts,shd->thd/dot_general | solution.py:114
  50.8 1.0 multiply_convert_fusion.7
  51.8 3.5 %collective-permute-start.2 = (bf16[128,16,128]{0,2,1:T(8,128)(2,1)}, bf16[128,16,128]{0,2,1:T(8,128)(2,1)}, u32[]{:S(2)}, u32[]{:S(2)}) collective-permute-start(bf16[128,16,128]{0,2,1:T(8,128)(2,1)} %multiply_convert_fusion.7), channel_id=1, source_target_pairs={{0,1},{1,0},{2,3},{3,2},{4,5},{5,4},{6,7},{7,6},{8,9},{9,8},{10,11... | collective-permute-start | bytes 1572872 | tf_op jit(solution)/shard_map/ppermute | solution.py:18
  55.3 1.2 copy.59
  56.7 24.1 %collective-permute-done.2 = bf16[128,16,128]{0,2,1:T(8,128)(2,1)} collective-permute-done((bf16[128,16,128]{0,2,1:T(8,128)(2,1)}, bf16[128,16,128]{0,2,1:T(8,128)(2,1)}, u32[]{:S(2)}, u32[]{:S(2)}) %collective-permute-start.2) | collective-permute-done | bytes 524320 | tf_op jit(solution)/shard_map/ppermute | solution.py:18
  80.7 3.6 %convert_add_fusion = f32[128,16,128]{0,2,1:T(8,128)} fusion(bf16[128,16,128]{0,2,1:T(8,128)(2,1)} %collective-permute-done.2, f32[128,16,128]{0,2,1:T(8,128)} %bitcast.110, f32[128,16]{0,1:T(8,128)S(1)} %broadcast_multiply_fusion.7, f32[128,16]{0,1:T(8,128)S(1)} %add_rsqrt_fusion.3, f32[256,16,128]{0,2,1:T(8,128)} %copy-done.2, ...), kind=kLoop, calls=%fused_computation.45 | loop fusion | flops 2359296 | bytes 5791744 | tf_op jit(solution)/shard_map/add | solution.py:142
  84.3 2.6 %copy.62 = f32[128,2048]{1,0:T(8,128)} copy(f32[128,2048]{0,1:T(8,128)} %bitcast.113) | data formatting | bytes 2097152 | tf_op jit(solution)/shard_map/reshape | solution.py:146
  86.9 11.7 %collective-permute-start.3 = (f32[128,2048]{1,0:T(8,128)}, f32[128,2048]{1,0:T(8,128)}, u32[]{:S(2)}, u32[]{:S(2)}) collective-permute-start(f32[128,2048]{1,0:T(8,128)} %copy.62), channel_id=1, source_target_pairs={{16,0},{32,16},{48,32},{64,48},{80,64},{96,80},{112,96},{128,112},... | collective-permute-start | bytes 3145736 | tf_op jit(solution)/shard_map/ppermute | solution.py:24
  98.6 1.1 broadcast_multiply_fusion
  99.7 4.8 %fusion.49 = (f32[16,128]{1,0:T(8,128)S(1)}, f32[16,128,256]{2,1,0:T(8,128)}) fusion(pred[256]{0:T(512)(128)(4,1)S(1)} %broadcast_bitcast_fusion, f32[16,128]{1,0:T(8,128)S(1)} %bitcast.126, f32[128,16,128]{0,2,1:T(8,128)} %broadcast_multiply_fusion, f32[128,16,128]{0,2,1:T(8,128)} %broadcast_multiply_fusion.1, f32[16,128]{1,0:T(8,128)S(1)} %bitcast.121), kind=kOutput, calls=%fused_computation.119 | convolution fusion | flops 138412288 | bytes 4219136 | tf_op jit(solution)/shard_map/sub | solution.py:66
  104.5 2.6 %fusion.12 = f32[16,128]{1,0:T(8,128)S(1)} fusion(f32[128,16,128]{0,2,1:T(8,128)S(1)} %bitcast.112, f32[16,128]{1,0:T(8,128)S(1)} %bitcast.133, f32[128,16,128]{0,2,1:T(8,128)S(1)} %copy-done.1, f32[128,16,128]{0,2,1:T(8,128)S(1)} %broadcast_multiply_fusion.3, f32[16,128,256]{2,1,0:T(8,128)} %get-tuple-element.24, f32[16,128]{1,0:T(8,128)S(1)} %get-tuple-element.23), kind=kOutput, calls=%fused_computation.37 | convolution fusion | flops 137361408 | bytes 5267456 | tf_op jit(solution)/shard_map/hts,shd->thd/dot_general | solution.py:69
  107.1 13.1 %collective-permute-done.3 = f32[128,2048]{1,0:T(8,128)} collective-permute-done((f32[128,2048]{1,0:T(8,128)}, f32[128,2048]{1,0:T(8,128)}, u32[]{:S(2)}, u32[]{:S(2)}) %collective-permute-start.3) | collective-permute-done | bytes 1048608 | tf_op jit(solution)/shard_map/ppermute | solution.py:24
  120.2 1.3 convert_select_fusion
  121.5 1.3 copy.63
  122.9 3.4 %multiply_reduce_fusion = (f32[16,128]{1,0:T(8,128)S(1)}, f32[16,128,256]{2,1,0:T(8,128)S(1)}) fusion(f32[16,128,256]{2,1,0:T(8,128)S(1)} %copy-done.6, f32[16,128]{1,0:T(8,128)S(1)} %get-tuple-element.28, f32[16,128]{1,0:T(8,128)S(1)} %bitcast.134, f32[128,16,128]{0,2,1:T(8,128)} %broadcast_multiply_fusion, f32[128,16,128]{0,2,1:T(8,128)} %broadcast_multiply_fusion.1, ...), kind=kOutput, calls=%fused_computation.17 | convolution fusion | flops 137885696 | bytes 7372800 | tf_op jit(solution)/shard_map/thd,shd->hts/dot_general | solution.py:71
  126.2 0.8 multiply_convert_fusion
  127.0 0.4 copy-done.7
  127.5 0.3 copy-done.8
  127.8 0.7 fusion.13
  128.5 0.7 fusion.3
  129.2 0.5 copy-done.9
  129.7 1.1 fusion.2
  130.8 1.2 fusion.14
  132.1 23.8 %psum.14 = f32[4,2048]{1,0:T(4,128)S(1)} all-reduce(f32[4,2048]{1,0:T(4,128)S(1)} %maximum_add_fusion), channel_id=1, replica_groups=mesh['segment'=32,'dp'=8,'seq'=2] {'dp'}, use_global_device_ids=true, to_apply=%region_22.23 | all-reduce | flops 8192 | bytes 65536 | tf_op jit(solution)/shard_map/psum | solution.py:152
  155.8 16.9 %psum.15 = f32[1,4,2048]{2,1,0:T(4,128)} all-reduce(f32[1,4,2048]{2,1,0:T(4,128)S(1)} %bitcast.117), channel_id=1, replica_groups=mesh['segment'=32,'dp'=8,'seq'=2] {'seq'}, use_global_device_ids=true, to_apply=%region_23.24 | all-reduce | flops 8192 | bytes 65536 | tf_op jit(solution)/shard_map/psum | solution.py:152
  (45 shorter events, 0.8 us)
Async XLA Ops:
  0.0 12.8 %copy-start.13 = (s32[1,2,1,2]{3,2,1,0:T(1,128)S(1)}, s32[1,2,1,2]{3,2,1,0:T(1,128)}, u32[]{:S(2)}) copy-start(s32[1,2,1,2]{3,2,1,0:T(1,128)} %param.11) | copy-start | bytes 52
  0.0 12.8 %copy-start.12 = (s32[1,2,1,2,2]{4,3,2,1,0:T(2,128)S(1)}, s32[1,2,1,2,2]{4,3,2,1,0:T(2,128)}, u32[]{:S(2)}) copy-start(s32[1,2,1,2,2]{4,3,2,1,0:T(2,128)} %param.10) | copy-start | bytes 100
  2.7 31.7 %collective-permute-start = (bf16[128,2048]{1,0:T(8,128)(2,1)}, bf16[128,2048]{1,0:T(8,128)(2,1)}, u32[]{:S(2)}, u32[]{:S(2)}) collective-permute-start(bf16[128,2048]{1,0:T(8,128)(2,1)} %get-tuple-element.12), channel_id=1, source_target_pairs={{0,1},{1,0},{2,3},{3,2},{4,5},{5,4},{6,7},{7,6},{8,9},{9,8},{10,11... | collective-permute-start | bytes 1572872 | tf_op jit(solution)/shard_map/ppermute | solution.py:18
  7.4 47.9 %collective-permute-start.1 = (bf16[128,2048]{1,0:T(8,128)(2,1)}, bf16[128,2048]{1,0:T(8,128)(2,1)}, u32[]{:S(2)}, u32[]{:S(2)}) collective-permute-start(bf16[128,2048]{1,0:T(8,128)(2,1)} %get-tuple-element.13), channel_id=1, source_target_pairs={{0,1},{1,0},{2,3},{3,2},{4,5},{5,4},{6,7},{7,6},{8,9},{9,8},{10,11... | collective-permute-start | bytes 1572872 | tf_op jit(solution)/shard_map/ppermute | solution.py:18
  14.0 0.8 copy-start.11
  40.8 2.9 %copy-start = (f32[128,16,128]{0,2,1:T(8,128)S(1)}, f32[128,16,128]{0,2,1:T(8,128)}, u32[]{:S(2)}) copy-start(f32[128,16,128]{0,2,1:T(8,128)} %broadcast_multiply_fusion.2) | copy-start | bytes 3145732
  40.8 2.9 %copy-start.3 = (f32[1,1,128,2048]{2,3,1,0:T(8,128)S(1)}, f32[1,1,128,2048]{2,3,1,0:T(8,128)}, u32[]{:S(2)}) copy-start(f32[1,1,128,2048]{2,3,1,0:T(8,128)} %copy.53) | copy-start | bytes 3145732
  40.8 3.2 %copy-start.5 = (f32[16,128,256]{2,1,0:T(8,128)S(1)}, f32[16,128,256]{2,1,0:T(8,128)}, u32[]{:S(2)}) copy-start(f32[16,128,256]{2,1,0:T(8,128)} %get-tuple-element.24) | copy-start | bytes 6291460
  48.8 1.9 %copy-start.2 = (f32[256,16,128]{0,2,1:T(8,128)}, f32[256,16,128]{0,2,1:T(8,128)S(1)}, u32[]{:S(2)}) copy-start(f32[256,16,128]{0,2,1:T(8,128)S(1)} %get-tuple-element.10) | copy-start | bytes 6291460
  51.8 29.0 %collective-permute-start.2 = (bf16[128,16,128]{0,2,1:T(8,128)(2,1)}, bf16[128,16,128]{0,2,1:T(8,128)(2,1)}, u32[]{:S(2)}, u32[]{:S(2)}) collective-permute-start(bf16[128,16,128]{0,2,1:T(8,128)(2,1)} %multiply_convert_fusion.7), channel_id=1, source_target_pairs={{0,1},{1,0},{2,3},{3,2},{4,5},{5,4},{6,7},{7,6},{8,9},{9,8},{10,11... | collective-permute-start | bytes 1572872 | tf_op jit(solution)/shard_map/ppermute | solution.py:18
  86.9 33.2 %collective-permute-start.3 = (f32[128,2048]{1,0:T(8,128)}, f32[128,2048]{1,0:T(8,128)}, u32[]{:S(2)}, u32[]{:S(2)}) collective-permute-start(f32[128,2048]{1,0:T(8,128)} %copy.62), channel_id=1, source_target_pairs={{16,0},{32,16},{48,32},{64,48},{80,64},{96,80},{112,96},{128,112},... | collective-permute-start | bytes 3145736 | tf_op jit(solution)/shard_map/ppermute | solution.py:24
  99.7 4.8 %copy-start.1 = (f32[128,16,128]{0,2,1:T(8,128)S(1)}, f32[128,16,128]{0,2,1:T(8,128)}, u32[]{:S(2)}) copy-start(f32[128,16,128]{0,2,1:T(8,128)} %broadcast_multiply_fusion.2) | copy-start | bytes 3145732
  99.7 4.8 %copy-start.4 = (f32[1,1,128,2048]{2,3,1,0:T(8,128)S(1)}, f32[1,1,128,2048]{2,3,1,0:T(8,128)}, u32[]{:S(2)}) copy-start(f32[1,1,128,2048]{2,3,1,0:T(8,128)} %copy.53) | copy-start | bytes 3145732
  104.5 15.7 %copy-start.10 = (bf16[1,1,128,2048]{3,2,1,0:T(8,128)(2,1)S(1)}, bf16[1,1,128,2048]{3,2,1,0:T(8,128)(2,1)}, u32[]{:S(2)}) copy-start(bf16[1,1,128,2048]{3,2,1,0:T(8,128)(2,1)} %param.8) | copy-start | bytes 1572868
  107.1 15.8 %copy-start.6 = (f32[16,128,256]{2,1,0:T(8,128)S(1)}, f32[16,128,256]{2,1,0:T(8,128)}, u32[]{:S(2)}) copy-start(f32[16,128,256]{2,1,0:T(8,128)} %get-tuple-element.29) | copy-start | bytes 6291460
  126.2 1.2 copy-start.7
  126.2 1.5 copy-start.8
  128.5 1.2 copy-start.9
